TPU v7x, 512 devices: a whole 4x8x8 slice. The times are simulated.
512 devices in a mesh: dom: 16 (over z, core), tile: 8 (over y), rep: 4 (over x).
Axes of the slice: x: 4, y: 8, z: 8, core: 2. Of those that a mesh axis runs over, the one named last changes fastest.
Arguments:
- quantizer_codes: int32 [131072, 32], P(('dom', 'tile', 'rep')), may hold values from 0 to 255
- codebook: bfloat16 [32, 256, 8], replicated, may hold values from -6 to 6
- adj_tiles: bfloat16 [512, 4, 256, 256], P(('dom', 'tile', 'rep')), may hold values from -0.3125 to 0.3125
- tile_list: int32 [512, 4, 2], P(('dom', 'tile', 'rep')), may hold values from 0 to 511, as said below
- tile_count: int32 [512], P(('dom', 'tile', 'rep')), may hold values from 1 to 4, as said below
- w_self: bfloat16 [256, 256], replicated, may hold values from -0.375 to 0.375
- w_neigh: bfloat16 [256, 256], replicated, may hold values from -0.375 to 0.375
- out_bias: float32 [256], replicated, may hold values from -3 to 3
- cotangent: bfloat16 [131072, 256], P(('dom', 'tile', 'rep')), may hold values from -0.15625 to 0.15625
Outputs:
- node_out: bfloat16 [131072, 256], P(('dom', 'tile', 'rep'))
- grad_self: float32 [256, 256], replicated
- grad_neigh: float32 [256, 256], replicated
- grad_bias: float32 [256], replicated
- grad_codebook: float32 [32, 256, 8], replicated
Inputs may be any that keep to these rules, and one draw needn't show every extreme that they name: `tile_list`: for device i (index along dom+tile+rep), every slot's row block r has r % 32 == i % 32 and its column block c has c // 32 == i // 32; slots at or beyond tile_count[i] are ignored. `tile_count`: some device has exactly 4 live slots.
All inputs are finite; a program needn't handle non-finite values.
Results may differ from a plain program's by a relative error of at most 0.0055.
Values may be sent and summed in bfloat16 or wider, within the bound.
No kernel may reach another device: no remote copies, remote signals or barrier semaphores. Data moves between devices by JAX's collectives and lax.ppermute only.
A program may use at most 192 MiB of HBM per device.

v0:
```python
import jax
import jax.numpy as jnp
from jax import lax
from jax.sharding import PartitionSpec as P

HIGH = lax.Precision.HIGHEST
CONTRACT_ROWS = (((0,), (0,)), ((), ()))
CONTRACT_COLS = (((1,), (1,)), ((), ()))


def finish(pre_act):
    hidden = jax.nn.silu(pre_act)
    return hidden * lax.rsqrt(jnp.mean(hidden * hidden, axis=-1, keepdims=True) + 1e-05)


def one_hot_codes(code_rows, centroids):
    centroid_ids = jnp.arange(centroids, dtype=jnp.int32)
    return (code_rows[:, :, None] == centroid_ids[None, None, :]).astype(jnp.bfloat16)


def body(
    quantizer_codes,
    codebook,
    adj_tiles,
    tile_list,
    tile_count,
    w_self,
    w_neigh,
    out_bias,
    cotangent,
):
    group_size = lax.axis_size("tile") * lax.axis_size("rep")
    dom_count = lax.axis_size("dom")
    sub_count, centroids, sub_width = codebook.shape
    tile_side = adj_tiles.shape[2]
    slot_total = adj_tiles.shape[1]
    feat_width = sub_count * sub_width
    tile_data = adj_tiles[0]
    row_dom = tile_list[0, :, 0] // group_size
    col_pos = tile_list[0, :, 1] % group_size
    live_count = tile_count[0]
    live_mask = jnp.arange(slot_total, dtype=jnp.int32) < live_count
    own_onehot = one_hot_codes(quantizer_codes, centroids)
    feats = jnp.einsum("nmk,mke->nme", own_onehot, codebook, preferred_element_type=jnp.float32)
    feats = feats.reshape(tile_side, feat_width).astype(jnp.bfloat16)
    gathered = lax.all_gather(feats, ("tile", "rep"), axis=0, tiled=True).reshape(
        group_size, tile_side, feat_width
    )
    chosen = jnp.take(gathered, col_pos, axis=0)
    products = jnp.einsum("sij,sjf->sif", tile_data, chosen, preferred_element_type=jnp.float32)
    targets = jnp.arange(lax.axis_size("dom") * tile_side // tile_side, dtype=jnp.int32)
    select = ((row_dom[None, :] == targets[:, None]) & live_mask[None, :]).astype(jnp.float32)
    summed = jnp.einsum("ds,sif->dif", select, products, precision=HIGH)
    aggregate = lax.psum_scatter(
        summed.reshape(lax.axis_size("dom") * tile_side, feat_width),
        "dom",
        scatter_dimension=0,
        tiled=True,
    ).astype(jnp.bfloat16)
    pre_act = (
        jnp.dot(feats, w_self, preferred_element_type=jnp.float32)
        + jnp.dot(aggregate, w_neigh, preferred_element_type=jnp.float32)
        + out_bias
    )
    out_full, pullback = jax.vjp(finish, pre_act)
    node_out = out_full.astype(jnp.bfloat16)
    dpre = pullback(cotangent.astype(jnp.float32))[0].astype(jnp.bfloat16)
    grad_self = lax.dot_general(feats, dpre, CONTRACT_ROWS, preferred_element_type=jnp.float32)
    grad_neigh = lax.dot_general(aggregate, dpre, CONTRACT_ROWS, preferred_element_type=jnp.float32)
    grad_bias = jnp.sum(dpre.astype(jnp.float32), axis=0)
    dx_self = lax.dot_general(dpre, w_self, CONTRACT_COLS, preferred_element_type=jnp.float32)
    dagg = lax.dot_general(dpre, w_neigh, CONTRACT_COLS, preferred_element_type=jnp.float32).astype(
        jnp.bfloat16
    )
    dagg_all = lax.all_gather(dagg, "dom", axis=0, tiled=True).reshape(
        dom_count, tile_side, feat_width
    )
    picked = jnp.take(dagg_all, row_dom, axis=0)
    backprod = jnp.einsum("sij,sif->sjf", tile_data, picked, preferred_element_type=jnp.float32)
    column_ids = jnp.arange(group_size, dtype=jnp.int32)
    select_cols = ((col_pos[None, :] == column_ids[:, None]) & live_mask[None, :]).astype(
        jnp.float32
    )
    column = jnp.einsum("gs,sjf->gjf", select_cols, backprod, precision=HIGH)
    column_low = column.astype(jnp.bfloat16)
    sub_dx = dx_self.reshape(tile_side, sub_count, sub_width)
    received = lax.all_to_all(column_low, ("tile", "rep"), split_axis=0, concat_axis=0, tiled=True)
    input_gradient_total = sub_dx + jnp.sum(received.astype(jnp.float32), axis=0).reshape(
        tile_side, sub_count, sub_width
    )
    grad_codebook = jnp.einsum(
        "nmk,nme->mke",
        own_onehot,
        input_gradient_total,
        precision=HIGH,
        preferred_element_type=jnp.float32,
    )
    grad_self, grad_neigh, grad_bias, grad_codebook = lax.psum(
        (grad_self, grad_neigh, grad_bias, grad_codebook), ("dom", "tile", "rep")
    )
    return (node_out, grad_self, grad_neigh, grad_bias, grad_codebook)


def solution(mesh):
    in_specs = (
        P(("dom", "tile", "rep"), None),
        P(),
        P(("dom", "tile", "rep"), None, None, None),
        P(("dom", "tile", "rep"), None, None),
        P(("dom", "tile", "rep")),
        P(),
        P(),
        P(),
        P(("dom", "tile", "rep"), None),
    )
    out_specs = (P(("dom", "tile", "rep"), None), P(), P(), P(), P())
    return jax.shard_map(body, mesh=mesh, in_specs=in_specs, out_specs=out_specs, check_vma=False)
```

profile of v0, /device:TPU:1, one launch (start us, length us, event | category | flops | bytes accessed | tf_op | source)
XLA Modules:
  0.0 638.8 jit_solution(5433840416255605811)
XLA Ops:
  7.2 3.2 fusion.7
  11.2 91.0 %all-gather.3.cloned.1.call-done = bf16[8192,256]{0,1:T(8,128)(2,1)} async-done(((bf16[256,256]{0,1:T(8,128)(2,1)}), bf16[8192,256]{0,1:T(8,128)(2,1)}) %all-gather.3.cloned.1.call-update) | async-done | bytes 4194320 | tf_op jit(solution)/shard_map/all_gather | solution.py:46
  102.2 6.4 %copy.20 = bf16[8192,256]{1,0:T(8,128)(2,1)} copy(bf16[8192,256]{0,1:T(8,128)(2,1)} %all-gather.3.cloned.1.call-done) | data formatting | bytes 8388608 | tf_op jit(solution)/shard_map/all_gather | solution.py:46
  108.7 2.8 gather_fusion
  112.3 2.0 fusion.26
  114.3 4.4 copy.23
  120.0 66.5 %reduce-scatter.2.cloned.1.call-done = f32[256,256]{1,0:T(8,128)} async-done(((f32[4096,256]{1,0:T(8,128)}), f32[256,256]{1,0:T(8,128)}) %reduce-scatter.2.cloned.1.call-update) | async-done | bytes 262160 | tf_op jit(solution)/shard_map/reduce_scatter | solution.py:54
  186.5 1.3 fusion.14
  188.0 0.9 convolution_convert_fusion.1
  188.9 44.4 %all-gather.5.cloned.1.call-done = bf16[4096,256]{1,0:T(8,128)(2,1)} async-done(((bf16[256,256]{1,0:T(8,128)(2,1)}), bf16[4096,256]{1,0:T(8,128)(2,1)}) %all-gather.5.cloned.1.call-update) | async-done | bytes 2097168 | tf_op jit(solution)/shard_map/all_gather | solution.py:75
  233.3 2.2 gather_fusion.1
  236.3 4.0 convolution_convert_fusion
  240.3 4.4 copy.27
  244.7 9.5 %all-to-all-start = ((bf16[32,256,256]{2,1,0:T(8,128)(2,1)}), bf16[32,256,256]{2,1,0:T(8,128)(2,1)}, u32[]{:S(2)}, u32[]{:S(2)}) async-start(bf16[32,256,256]{2,1,0:T(8,128)(2,1)} %copy.27), calls=%async_computation.1 | async-start | bytes 8388608 | tf_op jit(solution)/shard_map/all_to_all | solution.py:87
  254.3 0.9 fusion.44
  255.3 0.9 fusion.21
  256.2 91.6 %all-to-all-done = bf16[32,256,256]{2,1,0:T(8,128)(2,1)} async-done(((bf16[32,256,256]{2,1,0:T(8,128)(2,1)}), bf16[32,256,256]{2,1,0:T(8,128)(2,1)}, u32[]{:S(2)}, u32[]{:S(2)}) %all-to-all-start) | async-done | bytes 4194336 | tf_op jit(solution)/shard_map/all_to_all | solution.py:87
  347.7 2.8 convert_reduce_fusion
  350.9 3.8 fusion
  355.5 99.7 %psum.30 = f32[256]{0:T(256)} all-reduce(f32[256]{0:T(256)S(1)} %get-tuple-element.25), channel_id=1, replica_groups=mesh['dom'=16,'tile'=8,'rep'=4] {'dom','tile','rep'}, use_global_device_ids=true, to_apply=%region_6.7 | all-reduce | flops 256 | bytes 2048 | tf_op jit(solution)/shard_map/psum | solution.py:98
  455.2 172.1 %all-reduce.3.cloned.1.call-done = (f32[256,256]{1,0:T(8,128)}, f32[256,256]{1,0:T(8,128)}, f32[32,256,8]{1,2,0:T(8,128)}) async-done(((f32[256,256]{1,0:T(8,128)}, f32[256,256]{1,0:T(8,128)}, f32[32,256,8]{1,2,0:T(8,128)}), (f32[256,256]{1,0:T(8,128)}, f32[256,256]{1,0:T(8,128)}, f32[32,256,8]{1,2,0:T(8,128)})) %all-reduce.3.cloned.1.call-update) | async-done | bytes 786448 | tf_op jit(solution)/shard_map/psum | solution.py:98
  627.3 1.7 copy.38
  628.9 1.7 copy.39
  630.6 1.7 copy.40
  (41 shorter events, 4.4 us)
Async XLA Ops:
  7.2 104.3 %copy-start = (bf16[1,4,256,256]{3,2,1,0:T(8,128)(2,1)S(1)}, bf16[1,4,256,256]{3,2,1,0:T(8,128)(2,1)}, u32[]{:S(2)}) copy-start(bf16[1,4,256,256]{3,2,1,0:T(8,128)(2,1)} %param.11) | copy-start | bytes 1572868
  7.2 4.0 copy-start.6
  7.2 95.1 %all-gather.3.cloned.1.call-start = ((), (), s32[]{:S(2)}) async-start(), calls=%async_computation.2 | async-start | bytes 4325376 | tf_op jit(solution)/shard_map/all_gather | solution.py:46
  10.5 176.0 %reduce-scatter.2.cloned.1.call-start = ((), (), s32[]{:S(2)}) async-start(), calls=%async_computation.3 | async-start | bytes 4456448 | tf_op jit(solution)/shard_map/reduce_scatter | solution.py:54
  118.7 0.9 copy-start.5
  118.7 1.0 copy-start.1
  118.7 1.0 copy-start.2
  118.7 67.7 %copy-start.4 = (bf16[256,256]{1,0:T(8,128)(2,1)S(1)}, bf16[256,256]{1,0:T(8,128)(2,1)}, u32[]{:S(2)}) copy-start(bf16[256,256]{1,0:T(8,128)(2,1)} %param.15) | copy-start | bytes 393220
  118.7 67.7 %copy-start.8 = (f32[256]{0:T(256)S(1)}, f32[256]{0:T(256)}, u32[]{:S(2)}) copy-start(f32[256]{0:T(256)} %param.16) | copy-start | bytes 3076
  118.8 114.5 %all-gather.5.cloned.1.call-start = ((), (), s32[]{:S(2)}) async-start(), calls=%async_computation.4 | async-start | bytes 2228224 | tf_op jit(solution)/shard_map/all_gather | solution.py:75
  244.7 10.5 %copy-start.3 = (f32[256,256]{1,0:T(8,128)S(1)}, f32[256,256]{1,0:T(8,128)}, u32[]{:S(2)}) copy-start(f32[256,256]{1,0:T(8,128)} %reduce-scatter.2.cloned.1.call-done) | copy-start | bytes 786436
  244.7 103.0 %all-to-all-start = ((bf16[32,256,256]{2,1,0:T(8,128)(2,1)}), bf16[32,256,256]{2,1,0:T(8,128)(2,1)}, u32[]{:S(2)}, u32[]{:S(2)}) async-start(bf16[32,256,256]{2,1,0:T(8,128)(2,1)} %copy.27), calls=%async_computation.1 | async-start | bytes 8388608 | tf_op jit(solution)/shard_map/all_to_all | solution.py:87
  254.3 96.6 %copy-start.7 = (s32[256,32]{0,1:T(8,128)S(1)}, s32[256,32]{0,1:T(8,128)}, u32[]{:S(2)}) copy-start(s32[256,32]{0,1:T(8,128)} %param.9) | copy-start | bytes 98308
  254.3 373.0 %all-reduce.3.cloned.1.call-start = ((), (), s32[]{:S(2)}) async-start(), calls=%async_computation.5 | async-start | bytes 1572864 | tf_op jit(solution)/shard_map/psum | solution.py:98
Sparse Core Ops, SparseCore 0:
  11.6 90.5 all-gather.2
  118.9 67.5 reduce-scatter.1
  189.1 44.0 all-gather.4
  354.9 272.3 all-reduce.2
where the time goes:
time: 640 us; the launch traced here: 639 us
  waiting for transfers between devices  466 us (73%)
  blocking collectives  99.7 us (16%)
  local copies, waits for them, and re-layouts  27.6 us (4%)
  matrix products  18.4 us (3%)
  between operations  14.6 us (2%)
  starting transfers between devices  9.87 us (2%)
    psum x1, waiting for transfers between devices, body(): lax.psum((grad_self, grad_neigh, grad_bias, grad_codebook), ('dom', 'tile...  172 us
    psum x1, blocking collectives, body(): lax.psum((grad_self, grad_neigh, grad_bias, grad_codebook), ('dom', 'tile...  99.7 us
    all_to_all x1, waiting for transfers between devices, body(): lax.all_to_all(column_low, ('tile', 'rep'), split_axis=0, concat_axis=0,...  91.6 us
    all_gather x1, waiting for transfers between devices, body(): lax.all_gather(feats, ('tile', 'rep'), axis=0, tiled=True)  91 us
    reduce_scatter x1, waiting for transfers between devices, body(): lax.psum_scatter(summed.reshape(lax.axis_size('dom') * tile_side, feat_wi...  66.5 us
    all_gather x1, waiting for transfers between devices, body(): lax.all_gather(dagg, 'dom', axis=0, tiled=True)  44.4 us
  transfers between devices with their start and end apart: 5, of which 5 were waited for; matrix products, arithmetic and copies ran while one was open for 0% of the time, Pallas kernels for 0%

commit v1 on v0

v1 whole, which is shorter than its diff:
```python
import functools

import jax
import jax.numpy as jnp
from jax import lax
from jax.experimental import pallas as pl
from jax.experimental.pallas import tpu as pltpu
from jax.sharding import PartitionSpec as P

INTERPRET = False
F32 = jnp.float32
BF16 = jnp.bfloat16
VM = pltpu.VMEM
DOM = ("dom",)
PLANE = ("tile", "rep")


def contract(a, b, da, db):
    return lax.dot_general(a, b, (((da,), (db,)), ((), ())), preferred_element_type=F32)


def call(kernel, name, out_shape, scalars, arrays, scratch=()):
    return pl.pallas_call(
        kernel,
        name=name,
        out_shape=out_shape,
        in_specs=[pl.BlockSpec(memory_space=pltpu.SMEM)] * len(scalars)
        + [pl.BlockSpec(memory_space=VM)] * len(arrays),
        out_specs=jax.tree.map(lambda _: pl.BlockSpec(memory_space=VM), out_shape),
        scratch_shapes=list(scratch),
        interpret=INTERPRET,
    )(*scalars, *arrays)


def struct(shape, dtype):
    return jax.ShapeDtypeStruct(shape, dtype)


def onehot(row, centroid_ids):
    return jnp.where(centroid_ids == row, 1.0, 0.0).astype(BF16)


def centroid_iota(centroids, nodes):
    return lax.broadcasted_iota(jnp.int32, (centroids, nodes), 0).astype(F32)


def decode(codes, book_ref, ids, out_ref):
    sub_count, width, _ = book_ref.shape
    for m in range(sub_count):
        hot = onehot(codes[m : m + 1, :], ids)
        out_ref[m * width : (m + 1) * width, :] = jnp.dot(
            book_ref[m], hot, preferred_element_type=F32
        ).astype(out_ref.dtype)


def pack_kernel(tl_ref, tc_ref, codes_ref, cot_ref, spread_ref, side_ref):
    plane, subs, nodes = spread_ref.shape
    doms, rows2, width = side_ref.shape
    rows = rows2 // 2
    slots = tl_ref.shape[1]
    group = 128 // (slots * rows)
    codes = codes_ref[...].astype(F32).astype(BF16)
    spread_ref[...] = jnp.broadcast_to(codes[None], (plane, subs, nodes))
    eye = (
        lax.broadcasted_iota(jnp.int32, (subs, 128), 0)
        == lax.broadcasted_iota(jnp.int32, (subs, 128), 1)
    ).astype(F32)
    code_rows = contract(codes, eye.astype(BF16), 0, 0).astype(BF16)
    lane = lax.broadcasted_iota(jnp.int32, (rows, 128), 1)
    me = lax.axis_index("dom")
    at = lane - (me % group) * (slots * rows)
    slot = at // rows
    meta = jnp.zeros((rows, 128), jnp.int32)
    for s in range(slots):
        target = tl_ref[0, s] // plane * rows
        live = s < tc_ref[0]
        here = (at >= s * rows) & (at < (s + 1) * rows)
        meta = jnp.where(here, jnp.where(live, target + at - s * rows, nodes), meta)
    meta = meta.astype(F32).astype(BF16)
    for j in range(doms):
        side_ref[j, 0:rows, :] = cot_ref[j * rows : (j + 1) * rows, :]
        side_ref[j, rows:rows2, 0:128] = code_rows[j * rows : (j + 1) * rows, :]
        side_ref[j, rows:rows2, 128:256] = meta


def forward_kernel(tl_ref, adj_ref, codes_ref, book_ref, out_ref, feats_ref):
    plane = codes_ref.shape[0]
    doms = out_ref.shape[0]
    slots, side, _ = adj_ref.shape
    rows = side // doms
    ids = centroid_iota(book_ref.shape[2], codes_ref.shape[2])
    for s in range(slots):
        codes = codes_ref[tl_ref[1, s] % plane].astype(F32)
        decode(codes, book_ref, ids, feats_ref)
        prod = contract(adj_ref[s], feats_ref[...].astype(BF16), 1, 1).astype(BF16)
        for j in range(doms):
            out_ref[j, s * rows : (s + 1) * rows, :] = prod[j * rows : (j + 1) * rows, :]


def own_kernel(side_ref, book_ref, w_ref, bias_ref, feats_out, pre_ref, codes_out, feats_ref):
    doms, rows2, _ = side_ref.shape
    rows = rows2 // 2
    subs = book_ref.shape[0]
    code_rows = side_ref[:, rows:rows2, 0:128].reshape(doms * rows, 128)
    eye = (
        lax.broadcasted_iota(jnp.int32, (subs, 128), 0)
        == lax.broadcasted_iota(jnp.int32, (subs, 128), 1)
    ).astype(F32)
    codes = contract(eye.astype(BF16), code_rows, 1, 1)
    codes_out[...] = codes
    ids = centroid_iota(book_ref.shape[2], codes.shape[1])
    decode(codes, book_ref, ids, feats_ref)
    feats = feats_ref[...].astype(BF16)
    feats_out[...] = feats
    pre_ref[...] = contract(feats, w_ref[...], 0, 0) + bias_ref[...]


def node_kernel(side_ref, part_ref, pre_ref, w_ref, need_ref, node_ref, dpre_ref, agg_ref):
    doms, rows2, width = side_ref.shape
    rows = rows2 // 2
    per = part_ref.shape[1]
    group = 128 // per
    nodes = doms * rows
    row_ids = lax.broadcasted_iota(jnp.int32, (nodes, 128), 0).astype(F32)
    picks = []
    total = jnp.zeros((nodes, width), F32)
    for g in range(doms // group):
        meta = side_ref[g * group, rows : rows + 1, 128:256].astype(F32)
        for b in range(1, group):
            meta = meta + side_ref[g * group + b, rows : rows + 1, 128:256].astype(F32)
        pick = jnp.where(row_ids == meta, 1.0, 0.0).astype(BF16)
        picks.append(pick)
        terms = part_ref[g * group : (g + 1) * group].reshape(128, width)
        total = total + jnp.dot(pick, terms, preferred_element_type=F32)
    agg = total.astype(BF16)
    agg_ref[...] = agg
    pre = pre_ref[...] + jnp.dot(agg, w_ref[...], preferred_element_type=F32)
    gate = 1.0 / (1.0 + jnp.exp(-pre))
    hidden = pre * gate
    inv = lax.rsqrt(jnp.mean(hidden * hidden, axis=-1, keepdims=True) + 1e-05)
    node_ref[...] = (hidden * inv).astype(BF16).reshape(node_ref.shape)
    cot = side_ref[:, 0:rows, :].reshape(nodes, width).astype(F32)
    lean = jnp.mean(cot * hidden, axis=-1, keepdims=True) * (inv * inv * inv)
    dhidden = cot * inv - hidden * lean
    dpre = (dhidden * gate * (1.0 + pre * (1.0 - gate))).astype(BF16)
    dpre_ref[...] = dpre
    dagg = contract(dpre, w_ref[...], 1, 1).astype(BF16)
    for g in range(doms // group):
        need = contract(picks[g], dagg, 0, 0).astype(BF16)
        need_ref[g * group : (g + 1) * group] = need.reshape(group, per, width)


def weights_kernel(feats_ref, agg_ref, dpre_ref, w_ref, codes_ref, grads_ref, book_ref):
    plane, rows3, width = grads_ref.shape
    rows = rows3 - 8
    half = rows // 2
    dpre = dpre_ref[...]
    grad_self = jnp.dot(feats_ref[...], dpre, preferred_element_type=F32)
    grad_neigh = contract(agg_ref[...], dpre, 0, 0)
    bias = jnp.sum(dpre.astype(F32), axis=0, keepdims=True)
    for j in range(plane):
        grads_ref[j, 0:half, :] = grad_self[j * half : (j + 1) * half, :]
        grads_ref[j, half:rows, :] = grad_neigh[j * half : (j + 1) * half, :]
        grads_ref[j, rows:rows3, :] = jnp.broadcast_to(bias, (8, width))
    dx = contract(w_ref[...], dpre, 1, 1)
    subs, sub_width, centroids = book_ref.shape
    ids = centroid_iota(centroids, codes_ref.shape[1])
    high = dx.astype(BF16)
    low = (dx - high.astype(F32)).astype(BF16)
    for m in range(subs):
        hot = onehot(codes_ref[m : m + 1, :], ids)
        at = slice(m * sub_width, (m + 1) * sub_width)
        book_ref[m] = contract(high[at], hot, 1, 1) + contract(low[at], hot, 1, 1)


def backward_kernel(tl_ref, need_ref, adj_ref, codes_ref, own_ref, out_ref, dx_ref):
    plane = codes_ref.shape[0]
    slots, side, _ = adj_ref.shape
    subs, sub_width, centroids = out_ref.shape
    doms, per, width = need_ref.shape
    rows = per // slots
    ids = centroid_iota(centroids, codes_ref.shape[2])
    out_ref[...] = own_ref[...]
    for s in range(slots):
        dagg = need_ref[:, s * rows : (s + 1) * rows, :].reshape(side, width)
        dx_ref[...] = contract(dagg, adj_ref[s], 0, 0).astype(BF16).astype(F32)
        codes = codes_ref[tl_ref[1, s] % plane].astype(F32)
        for m in range(subs):
            hot = onehot(codes[m : m + 1, :], ids)
            dx = dx_ref[m * sub_width : (m + 1) * sub_width, :].astype(BF16)
            out_ref[m] += contract(dx, hot, 1, 1)


def sum_spread_kernel(in_ref, out_ref):
    total = jnp.sum(in_ref[...], axis=0)
    out_ref[...] = jnp.broadcast_to(total[None], out_ref.shape)


def exchange(x, axes):
    return lax.all_to_all(x, axes, split_axis=0, concat_axis=0, tiled=True)


def sum_everywhere(pieces, doms, name):
    plane = pieces.shape[0]
    tail = pieces.shape[1:]
    got = exchange(pieces, PLANE)
    got = exchange(call(sum_spread_kernel, name + "_a", struct((doms, *tail), F32), (), (got,)), DOM)
    got = call(sum_spread_kernel, name + "_b", struct((plane, *tail), F32), (), (got,))
    return exchange(got, PLANE)


def body(quantizer_codes, codebook, adj_tiles, tile_list, tile_count, w_self, w_neigh, out_bias, cotangent):
    doms = lax.axis_size("dom")
    plane = lax.axis_size("tile") * lax.axis_size("rep")
    subs, centroids, sub_width = codebook.shape
    slots, side = adj_tiles.shape[1:3]
    width = subs * sub_width
    rows = side // doms
    codes = quantizer_codes.T
    book = codebook.transpose(0, 2, 1)
    adj = adj_tiles[0]
    slot_ids = tile_list[0].T
    bias = out_bias.reshape(1, width)

    spread, side_pay = call(
        pack_kernel, "pack",
        (struct((plane, subs, side), BF16), struct((doms, 2 * rows, width), BF16)),
        (slot_ids, tile_count), (codes, cotangent),
    )
    all_codes = exchange(spread, PLANE)
    side_got = exchange(side_pay, DOM)
    parts = call(
        forward_kernel, "forward", struct((doms, slots * rows, width), BF16),
        (slot_ids,), (adj, all_codes, book), (VM((width, side), F32),),
    )
    parts = exchange(parts, DOM)
    feats, pre_self, own_codes = call(
        own_kernel, "own",
        (struct((width, side), BF16), struct((side, width), F32), struct((subs, side), F32)),
        (), (side_got, book, w_self, bias), (VM((width, side), F32),),
    )
    need, node, dpre, agg = call(
        node_kernel, "node",
        (struct((doms, slots * rows, width), BF16), struct((doms, rows, width), BF16),
         struct((side, width), BF16), struct((side, width), BF16)),
        (), (side_got, parts, pre_self, w_neigh),
    )
    need = exchange(need, DOM)
    half = width // plane
    grads, own_book = call(
        weights_kernel, "weights",
        (struct((plane, 2 * half + 8, width), F32), struct((subs, sub_width, centroids), F32)),
        (), (feats, agg, dpre, w_self, own_codes),
    )
    grads = sum_everywhere(grads, doms, "grads")
    book_part = call(
        backward_kernel, "backward", struct((subs, sub_width, centroids), F32),
        (slot_ids,), (need, adj, all_codes, own_book), (VM((width, side), F32),),
    )
    node_out = exchange(node, DOM).reshape(side, width)
    grad_book = sum_everywhere(
        book_part.reshape(plane, subs * sub_width // plane, centroids), doms, "book"
    ).reshape(subs, sub_width, centroids)
    grad_self = grads[:, 0:half, :].reshape(width, width)
    grad_neigh = grads[:, half : 2 * half, :].reshape(width, width)
    grad_bias = grads[0, 2 * half, :]
    return (node_out, grad_self, grad_neigh, grad_bias, grad_book.transpose(0, 2, 1))


def solution(mesh):
    every = ("dom", "tile", "rep")
    in_specs = (
        P(every, None), P(), P(every, None, None, None), P(every, None, None), P(every),
        P(), P(), P(), P(every, None),
    )
    out_specs = (P(every, None), P(), P(), P(), P())
    return jax.shard_map(body, mesh=mesh, in_specs=in_specs, out_specs=out_specs, check_vma=False)
```

time: 640 us -> 241 us (0.38)
  waiting for transfers between devices: 466 us -> 91.8 us
  blocking collectives: 99.7 us -> 64.6 us
  starting transfers between devices: 9.87 us -> 44.3 us
  Pallas kernels: 0 us -> 31.4 us
  local copies, waits for them, and re-layouts: 27.6 us -> 4.89 us
  matrix products: 18.4 us -> 0 us
  between operations: 14.6 us -> 1.35 us
    psum x1 -> x0, waiting for transfers between devices: 172 us -> none  [body(): lax.psum((grad_self, grad_neigh, grad_bias, grad_codebook), ('dom', 'tile...]
    all_gather x2 -> x0, waiting for transfers between devices: 135 us -> none  [the longest x1 91 us: body(): lax.all_gather(feats, ('tile', 'rep'), axis=0, tiled=True)]
    psum x1 -> x0, blocking collectives: 99.7 us -> none  [body(): lax.psum((grad_self, grad_neigh, grad_bias, grad_codebook), ('dom', 'tile...]
    reduce_scatter x1 -> x0, waiting for transfers between devices: 66.5 us -> none  [body(): lax.psum_scatter(summed.reshape(lax.axis_size('dom') * tile_side, feat_wi...]
    all_to_all x0 -> x3, blocking collectives: none -> 64.6 us  [exchange(): return lax.all_to_all(x, axes, split_axis=0, concat_axis=0, tiled=True)]
    all_to_all x1 -> x8, starting transfers between devices: 9.53 us -> 44.3 us  [exchange(): return lax.all_to_all(x, axes, split_axis=0, concat_axis=0, tiled=True)]
    pallas_call x0 -> x10, Pallas kernels: none -> 31.4 us  [call(): pl.pallas_call(kernel, name=name, out_shape=out_shape, in_specs=[pl.Block...]
    dot_general x12 -> x0, matrix products: 18.4 us -> none  [the longest x1 4.04 us: body(): column = jnp.einsum('gs,sjf->gjf', select_cols, backprod, precision=HIGH)]
  transfers between devices with their start and end apart: 5 -> 8, of which waited for: 5 -> 7; matrix products, arithmetic and copies ran while one was open for 0% -> 0% of each run, Pallas kernels for 0% -> 11%
where the time goes in v1:
time: 241 us; the launch traced here: 238 us
  waiting for transfers between devices  91.8 us (38%)
  blocking collectives  64.6 us (27%)
  starting transfers between devices  44.3 us (18%)
  Pallas kernels  31.4 us (13%)
  local copies, waits for them, and re-layouts  4.89 us (2%)
    all_to_all x8, waiting for transfers between devices, exchange(): return lax.all_to_all(x, axes, split_axis=0, concat_axis=0, tiled=True)  91.8 us
    all_to_all x3, blocking collectives, exchange(): return lax.all_to_all(x, axes, split_axis=0, concat_axis=0, tiled=True)  64.6 us
    all_to_all x8, starting transfers between devices, exchange(): return lax.all_to_all(x, axes, split_axis=0, concat_axis=0, tiled=True)  44.3 us
    pallas_call x10, Pallas kernels, call(): pl.pallas_call(kernel, name=name, out_shape=out_shape, in_specs=[pl.Block...  31.4 us
  transfers between devices with their start and end apart: 8, of which 7 were waited for; matrix products, arithmetic and copies ran while one was open for 0% of the time, Pallas kernels for 11%

profile of v1, /device:TPU:1, one launch (start us, length us, event | category | flops | bytes accessed | tf_op | source)
XLA Modules:
  0.0 238.4 jit_solution(5448012652479896354)
XLA Ops:
  3.1 26.9 %all_to_all.55.codes_ref = bf16[32,32,256]{2,1,0:T(8,128)(2,1)} all-to-all(bf16[32,32,256]{2,1,0:T(8,128)(2,1)} %get-tuple-element.17), channel_id=1, replica_groups=mesh['dom'=16,'tile'=8,'rep'=4] {'tile','rep'}, dimensions={0} | all-to-all | bytes 1048576 | tf_op jit(solution)/shard_map/all_to_all | solution.py:200
  30.0 12.8 %all-to-all-start = ((bf16[16,32,256]{2,1,0:T(8,128)(2,1)}), bf16[16,32,256]{2,1,0:T(8,128)(2,1)S(1)}, u32[]{:S(2)}, u32[]{:S(2)}) async-start(bf16[16,32,256]{2,1,0:T(8,128)(2,1)} %get-tuple-element.16), calls=%async_computation | async-start | bytes 524288 | tf_op jit(solution)/shard_map/all_to_all | solution.py:200
  42.8 4.9 %forward.1 = bf16[16,64,256]{2,1,0:T(8,128)(2,1)} custom-call(s32[2,4]{1,0:T(2,128)} %bitcast.22, bf16[4,256,256]{2,1,0:T(8,128)(2,1)} %bitcast.14, bf16[32,32,256]{2,1,0:T(8,128)(2,1)} %all_to_all.55.codes_ref, bf16[32,8,256]{2,1,0:T(8,128)(2,1)} %bitcast.17), custom_call_target="tpu_custom_call" | custom-call | tf_op jit(solution)/shard_map/forward/pallas_call | solution.py:23
  47.7 6.7 %all-to-all-done.side_ref = bf16[16,32,256]{2,1,0:T(8,128)(2,1)S(1)} async-done(((bf16[16,32,256]{2,1,0:T(8,128)(2,1)}), bf16[16,32,256]{2,1,0:T(8,128)(2,1)S(1)}, u32[]{:S(2)}, u32[]{:S(2)}) %all-to-all-start) | async-done | bytes 262176 | tf_op jit(solution)/shard_map/all_to_all | solution.py:200
  55.1 3.5 %all-to-all-start.2 = ((bf16[16,64,256]{2,1,0:T(8,128)(2,1)}), bf16[16,64,256]{2,1,0:T(8,128)(2,1)S(1)}, u32[]{:S(2)}, u32[]{:S(2)}) async-start(bf16[16,64,256]{2,1,0:T(8,128)(2,1)} %forward.1), calls=%async_computation.2 | async-start | bytes 1048576 | tf_op jit(solution)/shard_map/all_to_all | solution.py:200
  58.5 2.8 %own.1 = (bf16[256,256]{1,0:T(8,128)(2,1)}, f32[256,256]{1,0:T(8,128)}, f32[32,256]{1,0:T(8,128)}) custom-call(bf16[16,32,256]{2,1,0:T(8,128)(2,1)} %copy-done.1, bf16[32,8,256]{2,1,0:T(8,128)(2,1)} %bitcast.18, bf16[256,256]{1,0:T(8,128)(2,1)} %w_ref.5, f32[1,256]{1,0:T(1,128)} %bitcast.24), custom_call_target="tpu_custom_call" | custom-call | tf_op jit(solution)/shard_map/own/pallas_call | solution.py:23
  61.4 13.9 %all-to-all-done.2.part_ref = bf16[16,64,256]{2,1,0:T(8,128)(2,1)S(1)} async-done(((bf16[16,64,256]{2,1,0:T(8,128)(2,1)}), bf16[16,64,256]{2,1,0:T(8,128)(2,1)S(1)}, u32[]{:S(2)}, u32[]{:S(2)}) %all-to-all-start.2) | async-done | bytes 524320 | tf_op jit(solution)/shard_map/all_to_all | solution.py:200
  76.1 3.4 %node.1 = (bf16[16,64,256]{2,1,0:T(8,128)(2,1)}, bf16[16,16,256]{2,1,0:T(8,128)(2,1)}, bf16[256,256]{1,0:T(8,128)(2,1)}, bf16[256,256]{1,0:T(8,128)(2,1)}) custom-call(bf16[16,32,256]{2,1,0:T(8,128)(2,1)} %copy-done.1, bf16[16,64,256]{2,1,0:T(8,128)(2,1)} %copy-done.2, f32[256,256]{1,0:T(8,128)} %get-tuple-element.18.pre_ref, bf16[256,256]{1,0:T(8,128)(2,1)} %w_ref.4), custom_call_target="tpu_custom_call" | custom-call | tf_op jit(solution)/shard_map/node/pallas_call | solution.py:23
  79.5 20.4 %all_to_all.56.need_ref = bf16[16,64,256]{2,1,0:T(8,128)(2,1)} all-to-all(bf16[16,64,256]{2,1,0:T(8,128)(2,1)} %get-tuple-element.25), channel_id=1, replica_groups=mesh['dom'=16,'tile'=8,'rep'=4] {'dom'}, dimensions={0} | all-to-all | bytes 1048576 | tf_op jit(solution)/shard_map/all_to_all | solution.py:200
  99.9 3.4 %all-to-all-start.3 = ((bf16[16,16,256]{2,1,0:T(8,128)(2,1)}), bf16[16,16,256]{2,1,0:T(8,128)(2,1)S(1)}, u32[]{:S(2)}, u32[]{:S(2)}) async-start(bf16[16,16,256]{2,1,0:T(8,128)(2,1)} %get-tuple-element.19), calls=%async_computation.3 | async-start | bytes 262144 | tf_op jit(solution)/shard_map/all_to_all | solution.py:200
  103.3 4.3 %weights.1 = (f32[32,24,256]{2,1,0:T(8,128)}, f32[32,8,256]{2,1,0:T(8,128)}) custom-call(bf16[256,256]{1,0:T(8,128)(2,1)} %get-tuple-element.20.feats_ref, bf16[256,256]{1,0:T(8,128)(2,1)} %get-tuple-element.21.agg_ref, bf16[256,256]{1,0:T(8,128)(2,1)} %get-tuple-element.22.dpre_ref, bf16[256,256]{1,0:T(8,128)(2,1)} %w_ref.5, ...), custom_call_target="tpu_custom_call" | custom-call | tf_op jit(solution)/shard_map/weights/pallas_call | solution.py:23
  107.6 6.9 %backward.1 = f32[32,8,256]{2,1,0:T(8,128)} custom-call(s32[2,4]{1,0:T(2,128)} %bitcast.23, bf16[16,64,256]{2,1,0:T(8,128)(2,1)} %all_to_all.56.need_ref, bf16[4,256,256]{2,1,0:T(8,128)(2,1)} %bitcast.15, bf16[32,32,256]{2,1,0:T(8,128)(2,1)} %all_to_all.55.codes_ref, f32[32,8,256]{2,1,0:T(8,128)} %get-tuple-element.26.own_ref), custom_call_target="tpu_custom_call" | custom-call | tf_op jit(solution)/shard_map/backward/pallas_call | solution.py:23
  114.5 17.3 %all_to_all.57.in_ref = f32[32,8,256]{2,1,0:T(8,128)} all-to-all(f32[32,8,256]{2,1,0:T(8,128)} %backward.1), channel_id=1, replica_groups=mesh['dom'=16,'tile'=8,'rep'=4] {'tile','rep'}, dimensions={0} | all-to-all | bytes 524288 | tf_op jit(solution)/shard_map/all_to_all | solution.py:200
  131.9 3.9 %all-to-all-start.4 = ((f32[32,24,256]{2,1,0:T(8,128)}), f32[32,24,256]{2,1,0:T(8,128)S(1)}, u32[]{:S(2)}, u32[]{:S(2)}) async-start(f32[32,24,256]{2,1,0:T(8,128)} %get-tuple-element.24), calls=%async_computation.4 | async-start | bytes 1572864 | tf_op jit(solution)/shard_map/all_to_all | solution.py:200
  137.4 19.4 %all-to-all-done.4.in_ref = f32[32,24,256]{2,1,0:T(8,128)S(1)} async-done(((f32[32,24,256]{2,1,0:T(8,128)}), f32[32,24,256]{2,1,0:T(8,128)S(1)}, u32[]{:S(2)}, u32[]{:S(2)}) %all-to-all-start.4) | async-done | bytes 786464 | tf_op jit(solution)/shard_map/all_to_all | solution.py:200
  156.8 8.3 %all-to-all-start.9 = ((f32[16,8,256]{2,1,0:T(8,128)}), f32[16,8,256]{2,1,0:T(8,128)S(1)}, u32[]{:S(2)}, u32[]{:S(2)}) async-start(f32[16,8,256]{2,1,0:T(8,128)} %book_a.1), calls=%async_computation.9 | async-start | bytes 262144 | tf_op jit(solution)/shard_map/all_to_all | solution.py:200
  165.1 2.0 grads_a.1
  167.1 6.9 %all-to-all-done.9.in_ref = f32[16,8,256]{2,1,0:T(8,128)S(1)} async-done(((f32[16,8,256]{2,1,0:T(8,128)}), f32[16,8,256]{2,1,0:T(8,128)S(1)}, u32[]{:S(2)}, u32[]{:S(2)}) %all-to-all-start.9) | async-done | bytes 131104 | tf_op jit(solution)/shard_map/all_to_all | solution.py:200
  174.7 3.4 %all-to-all-start.5 = ((f32[16,24,256]{2,1,0:T(8,128)}), f32[16,24,256]{2,1,0:T(8,128)S(1)}, u32[]{:S(2)}, u32[]{:S(2)}) async-start(f32[16,24,256]{2,1,0:T(8,128)} %grads_a.1), calls=%async_computation.5 | async-start | bytes 786432 | tf_op jit(solution)/shard_map/all_to_all | solution.py:200
  179.8 12.7 %all-to-all-done.5.in_ref = f32[16,24,256]{2,1,0:T(8,128)S(1)} async-done(((f32[16,24,256]{2,1,0:T(8,128)}), f32[16,24,256]{2,1,0:T(8,128)S(1)}, u32[]{:S(2)}, u32[]{:S(2)}) %all-to-all-start.5) | async-done | bytes 393248 | tf_op jit(solution)/shard_map/all_to_all | solution.py:200
  192.5 5.0 %all-to-all-start.10 = ((f32[32,8,256]{2,1,0:T(8,128)}), f32[32,8,256]{2,1,0:T(8,128)S(1)}, u32[]{:S(2)}, u32[]{:S(2)}) async-start(f32[32,8,256]{2,1,0:T(8,128)} %book_b.1), calls=%async_computation.10 | async-start | bytes 524288 | tf_op jit(solution)/shard_map/all_to_all | solution.py:200
  199.5 11.0 %all-to-all-done.10 = f32[32,8,256]{2,1,0:T(8,128)S(1)} async-done(((f32[32,8,256]{2,1,0:T(8,128)}), f32[32,8,256]{2,1,0:T(8,128)S(1)}, u32[]{:S(2)}, u32[]{:S(2)}) %all-to-all-start.10) | async-done | bytes 262176 | tf_op jit(solution)/shard_map/all_to_all | solution.py:200
  210.5 3.9 %all-to-all-start.6 = ((f32[32,24,256]{2,1,0:T(8,128)}), f32[32,24,256]{2,1,0:T(8,128)S(1)}, u32[]{:S(2)}, u32[]{:S(2)}) async-start(f32[32,24,256]{2,1,0:T(8,128)} %grads_b.1), calls=%async_computation.6 | async-start | bytes 1572864 | tf_op jit(solution)/shard_map/all_to_all | solution.py:200
  214.4 21.2 %all-to-all-done.6 = f32[32,24,256]{2,1,0:T(8,128)S(1)} async-done(((f32[32,24,256]{2,1,0:T(8,128)}), f32[32,24,256]{2,1,0:T(8,128)S(1)}, u32[]{:S(2)}, u32[]{:S(2)}) %all-to-all-start.6) | async-done | bytes 786464 | tf_op jit(solution)/shard_map/all_to_all | solution.py:200
  (19 shorter events, 12.0 us)
Async XLA Ops:
  30.0 24.3 %all-to-all-start = ((bf16[16,32,256]{2,1,0:T(8,128)(2,1)}), bf16[16,32,256]{2,1,0:T(8,128)(2,1)S(1)}, u32[]{:S(2)}, u32[]{:S(2)}) async-start(bf16[16,32,256]{2,1,0:T(8,128)(2,1)} %get-tuple-element.16), calls=%async_computation | async-start | bytes 524288 | tf_op jit(solution)/shard_map/all_to_all | solution.py:200
  54.4 0.7 copy-start.1
  55.1 20.2 %all-to-all-start.2 = ((bf16[16,64,256]{2,1,0:T(8,128)(2,1)}), bf16[16,64,256]{2,1,0:T(8,128)(2,1)S(1)}, u32[]{:S(2)}, u32[]{:S(2)}) async-start(bf16[16,64,256]{2,1,0:T(8,128)(2,1)} %forward.1), calls=%async_computation.2 | async-start | bytes 1048576 | tf_op jit(solution)/shard_map/all_to_all | solution.py:200
  75.3 0.8 copy-start.2
  99.9 14.6 %all-to-all-start.3 = ((bf16[16,16,256]{2,1,0:T(8,128)(2,1)}), bf16[16,16,256]{2,1,0:T(8,128)(2,1)S(1)}, u32[]{:S(2)}, u32[]{:S(2)}) async-start(bf16[16,16,256]{2,1,0:T(8,128)(2,1)} %get-tuple-element.19), calls=%async_computation.3 | async-start | bytes 262144 | tf_op jit(solution)/shard_map/all_to_all | solution.py:200
  131.9 24.9 %all-to-all-start.4 = ((f32[32,24,256]{2,1,0:T(8,128)}), f32[32,24,256]{2,1,0:T(8,128)S(1)}, u32[]{:S(2)}, u32[]{:S(2)}) async-start(f32[32,24,256]{2,1,0:T(8,128)} %get-tuple-element.24), calls=%async_computation.4 | async-start | bytes 1572864 | tf_op jit(solution)/shard_map/all_to_all | solution.py:200
  156.8 8.3 %copy-start = (f32[32,24,256]{2,1,0:T(8,128)}, f32[32,24,256]{2,1,0:T(8,128)S(1)}, u32[]{:S(2)}) copy-start(f32[32,24,256]{2,1,0:T(8,128)S(1)} %all-to-all-done.4.in_ref) | copy-start | bytes 2359300
  156.8 17.2 %all-to-all-start.9 = ((f32[16,8,256]{2,1,0:T(8,128)}), f32[16,8,256]{2,1,0:T(8,128)S(1)}, u32[]{:S(2)}, u32[]{:S(2)}) async-start(f32[16,8,256]{2,1,0:T(8,128)} %book_a.1), calls=%async_computation.9 | async-start | bytes 262144 | tf_op jit(solution)/shard_map/all_to_all | solution.py:200
  174.0 0.7 copy-start.4
  174.7 17.8 %all-to-all-start.5 = ((f32[16,24,256]{2,1,0:T(8,128)}), f32[16,24,256]{2,1,0:T(8,128)S(1)}, u32[]{:S(2)}, u32[]{:S(2)}) async-start(f32[16,24,256]{2,1,0:T(8,128)} %grads_a.1), calls=%async_computation.5 | async-start | bytes 786432 | tf_op jit(solution)/shard_map/all_to_all | solution.py:200
  192.5 5.1 %copy-start.3 = (f32[16,24,256]{2,1,0:T(8,128)}, f32[16,24,256]{2,1,0:T(8,128)S(1)}, u32[]{:S(2)}) copy-start(f32[16,24,256]{2,1,0:T(8,128)S(1)} %all-to-all-done.5.in_ref) | copy-start | bytes 1179652
  192.5 18.0 %all-to-all-start.10 = ((f32[32,8,256]{2,1,0:T(8,128)}), f32[32,8,256]{2,1,0:T(8,128)S(1)}, u32[]{:S(2)}, u32[]{:S(2)}) async-start(f32[32,8,256]{2,1,0:T(8,128)} %book_b.1), calls=%async_computation.10 | async-start | bytes 524288 | tf_op jit(solution)/shard_map/all_to_all | solution.py:200
  210.5 25.1 %all-to-all-start.6 = ((f32[32,24,256]{2,1,0:T(8,128)}), f32[32,24,256]{2,1,0:T(8,128)S(1)}, u32[]{:S(2)}, u32[]{:S(2)}) async-start(f32[32,24,256]{2,1,0:T(8,128)} %grads_b.1), calls=%async_computation.6 | async-start | bytes 1572864 | tf_op jit(solution)/shard_map/all_to_all | solution.py:200

commit v2 on v1

v2 whole, which is shorter than its diff:
```python
import functools

import jax
import jax.numpy as jnp
from jax import lax
from jax.experimental import pallas as pl
from jax.experimental.pallas import tpu as pltpu
from jax.sharding import PartitionSpec as P

INTERPRET = False
F32 = jnp.float32
BF16 = jnp.bfloat16
VM = pltpu.VMEM
DOM = ("dom",)
PLANE = ("tile", "rep")


def contract(a, b, da, db):
    return lax.dot_general(a, b, (((da,), (db,)), ((), ())), preferred_element_type=F32)


def call(kernel, name, out_shape, scalars, arrays, scratch=()):
    return pl.pallas_call(
        kernel,
        name=name,
        out_shape=out_shape,
        in_specs=[pl.BlockSpec(memory_space=pltpu.SMEM)] * len(scalars)
        + [pl.BlockSpec(memory_space=VM)] * len(arrays),
        out_specs=jax.tree.map(lambda _: pl.BlockSpec(memory_space=VM), out_shape),
        scratch_shapes=list(scratch),
        interpret=INTERPRET,
    )(*scalars, *arrays)


def struct(shape, dtype):
    return jax.ShapeDtypeStruct(shape, dtype)


def onehot(row, centroid_ids):
    return jnp.where(centroid_ids == row, 1.0, 0.0).astype(BF16)


def centroid_iota(centroids, nodes):
    return lax.broadcasted_iota(jnp.int32, (centroids, nodes), 0).astype(F32)


def decode(codes, book_ref, ids, out_ref):
    sub_count, width, _ = book_ref.shape
    for m in range(sub_count):
        hot = onehot(codes[m : m + 1, :], ids)
        out_ref[m * width : (m + 1) * width, :] = jnp.dot(
            book_ref[m], hot, preferred_element_type=F32
        ).astype(out_ref.dtype)


def side_kernel(plane, tl_ref, tc_ref, codes_ref, cot_ref, side_ref):
    doms, rows2, width = side_ref.shape
    rows = rows2 // 2
    subs, nodes = codes_ref.shape
    slots = tl_ref.shape[1]
    group = 128 // (slots * rows)
    codes = codes_ref[...].astype(F32).astype(BF16)
    eye = (
        lax.broadcasted_iota(jnp.int32, (subs, 128), 0)
        == lax.broadcasted_iota(jnp.int32, (subs, 128), 1)
    ).astype(F32)
    code_rows = contract(codes, eye.astype(BF16), 0, 0).astype(BF16)
    at = lax.broadcasted_iota(jnp.int32, (rows, 128), 1)
    at = at - (lax.axis_index("dom") % group) * (slots * rows)
    meta = jnp.zeros((rows, 128), jnp.int32)
    for s in range(slots):
        target = tl_ref[0, s] // plane * rows
        here = (at >= s * rows) & (at < (s + 1) * rows)
        live = s < tc_ref[0]
        meta = jnp.where(here, jnp.where(live, target + at - s * rows, nodes), meta)
    meta = meta.astype(F32).astype(BF16)
    for j in range(doms):
        side_ref[j, 0:rows, :] = cot_ref[j * rows : (j + 1) * rows, :]
        side_ref[j, rows:rows2, 0:128] = code_rows[j * rows : (j + 1) * rows, :]
        side_ref[j, rows:rows2, 128:256] = meta


def forward_kernel(tl_ref, adj_ref, codes_ref, book_ref, side_ref, out_ref, feats_ref):
    plane = codes_ref.shape[0]
    doms = out_ref.shape[0]
    slots, side, _ = adj_ref.shape
    rows = side // doms
    ids = centroid_iota(book_ref.shape[2], codes_ref.shape[2])
    for s in range(slots):
        codes = codes_ref[tl_ref[1, s] % plane].astype(F32)
        decode(codes, book_ref, ids, feats_ref)
        prod = contract(adj_ref[s], feats_ref[...].astype(BF16), 1, 1).astype(BF16)
        for j in range(doms):
            out_ref[j, s * rows : (s + 1) * rows, :] = prod[j * rows : (j + 1) * rows, :]
    out_ref[:, slots * rows :, :] = side_ref[...]


def node_kernel(
    got_ref, book_ref, wself_ref, wneigh_ref, bias_ref,
    send_ref, dpre_ref, agg_ref, feats_out, codes_out, feats_ref,
):
    doms, all_rows, width = got_ref.shape
    per = all_rows * 2 // 3
    rows = (all_rows - per) // 2
    group = 128 // per
    nodes = doms * rows
    subs = book_ref.shape[0]
    code_rows = got_ref[:, per + rows :, 0:128].reshape(nodes, 128)
    eye = (
        lax.broadcasted_iota(jnp.int32, (subs, 128), 0)
        == lax.broadcasted_iota(jnp.int32, (subs, 128), 1)
    ).astype(F32)
    codes = contract(eye.astype(BF16), code_rows, 1, 1)
    codes_out[...] = codes
    decode(codes, book_ref, centroid_iota(book_ref.shape[2], nodes), feats_ref)
    feats = feats_ref[...].astype(BF16)
    feats_out[...] = feats

    row_ids = lax.broadcasted_iota(jnp.int32, (nodes, 128), 0).astype(F32)
    picks = []
    total = jnp.zeros((nodes, width), F32)
    at = per + rows
    for g in range(doms // group):
        meta = got_ref[g * group, at : at + 1, 128:256].astype(F32)
        for b in range(1, group):
            meta = meta + got_ref[g * group + b, at : at + 1, 128:256].astype(F32)
        pick = jnp.where(row_ids == meta, 1.0, 0.0).astype(BF16)
        picks.append(pick)
        terms = got_ref[g * group : (g + 1) * group, 0:per, :].reshape(128, width)
        total = total + jnp.dot(pick, terms, preferred_element_type=F32)
    agg = total.astype(BF16)
    agg_ref[...] = agg
    pre = (
        contract(feats, wself_ref[...], 0, 0)
        + jnp.dot(agg, wneigh_ref[...], preferred_element_type=F32)
        + bias_ref[...]
    )
    gate = 1.0 / (1.0 + jnp.exp(-pre))
    hidden = pre * gate
    inv = lax.rsqrt(jnp.mean(hidden * hidden, axis=-1, keepdims=True) + 1e-05)
    send_ref[:, per:, :] = (hidden * inv).astype(BF16).reshape(doms, rows, width)
    cot = got_ref[:, per : per + rows, :].reshape(nodes, width).astype(F32)
    lean = jnp.mean(cot * hidden, axis=-1, keepdims=True) * (inv * inv * inv)
    dhidden = cot * inv - hidden * lean
    dpre = (dhidden * gate * (1.0 + pre * (1.0 - gate))).astype(BF16)
    dpre_ref[...] = dpre
    dagg = contract(dpre, wneigh_ref[...], 1, 1).astype(BF16)
    for g in range(doms // group):
        need = contract(picks[g], dagg, 0, 0).astype(BF16)
        send_ref[g * group : (g + 1) * group, 0:per, :] = need.reshape(group, per, width)


def weights_kernel(feats_ref, agg_ref, dpre_ref, w_ref, codes_ref, self_ref, neigh_ref, bias_ref, book_ref):
    dpre = dpre_ref[...]
    self_ref[...] = jnp.dot(feats_ref[...], dpre, preferred_element_type=F32)
    neigh_ref[...] = contract(agg_ref[...], dpre, 0, 0)
    bias = jnp.sum(dpre.astype(F32), axis=0, keepdims=True)
    bias_ref[...] = jnp.broadcast_to(bias, bias_ref.shape)
    dx = contract(w_ref[...], dpre, 1, 1)
    subs, sub_width, centroids = book_ref.shape
    ids = centroid_iota(centroids, codes_ref.shape[1])
    high = dx.astype(BF16)
    low = (dx - high.astype(F32)).astype(BF16)
    for m in range(subs):
        hot = onehot(codes_ref[m : m + 1, :], ids)
        at = slice(m * sub_width, (m + 1) * sub_width)
        book_ref[m] = contract(high[at], hot, 1, 1) + contract(low[at], hot, 1, 1)


def backward_kernel(
    tl_ref, got_ref, adj_ref, codes_ref, own_ref, self_ref, neigh_ref, bias_ref,
    keep_ref, give_ref, node_ref, dx_ref, book_ref,
):
    plane = codes_ref.shape[0]
    slots, side, _ = adj_ref.shape
    subs, sub_width, centroids = own_ref.shape
    doms, all_rows, width = got_ref.shape
    rows = side // doms
    per = slots * rows
    ids = centroid_iota(centroids, codes_ref.shape[2])
    book_ref[...] = own_ref[...]
    for s in range(slots):
        dagg = got_ref[:, s * rows : (s + 1) * rows, :].reshape(side, width)
        dx_ref[...] = contract(dagg, adj_ref[s], 0, 0).astype(BF16).astype(F32)
        codes = codes_ref[tl_ref[1, s] % plane].astype(F32)
        for m in range(subs):
            hot = onehot(codes[m : m + 1, :], ids)
            dx = dx_ref[m * sub_width : (m + 1) * sub_width, :].astype(BF16)
            book_ref[m] += contract(dx, hot, 1, 1)
    node_ref[...] = got_ref[:, per:, :].reshape(side, width)
    core = lax.axis_index("dom") % 2
    pieces = keep_ref.shape[0]
    half = width // pieces
    each = subs // pieces
    low = lax.broadcasted_iota(jnp.int32, (sub_width, centroids), 0) < sub_width // 2
    bias = bias_ref[...]

    def write(first_ref, second_ref):
        for j in range(pieces):
            first_ref[j, 0:half, :] = self_ref[j * half : (j + 1) * half, :]
            second_ref[j, 0:half, :] = neigh_ref[j * half : (j + 1) * half, :]
            for e in range(each):
                at = slice(half + e * sub_width, half + (e + 1) * sub_width)
                value = book_ref[j * each + e]
                first_ref[j, at, :] = jnp.where(low, value, bias)
                second_ref[j, at, :] = jnp.where(low, 0.0, value)

    @pl.when(core == 0)
    def _():
        write(keep_ref, give_ref)

    @pl.when(core == 1)
    def _():
        write(give_ref, keep_ref)


def pair_kernel(keep_ref, got_ref, out_ref):
    out_ref[...] = (keep_ref[...] + got_ref[...]).astype(out_ref.dtype)


def sum_spread_kernel(in_ref, out_ref):
    total = jnp.sum(in_ref[...].astype(F32), axis=0)
    out_ref[...] = jnp.broadcast_to(total[None].astype(out_ref.dtype), out_ref.shape)


def finish_kernel(mine_ref, other_ref, self_ref, neigh_ref, bias_ref, book_ref):
    core = lax.axis_index("dom") % 2
    pieces = mine_ref.shape[0]
    half = self_ref.shape[0] // pieces
    subs, sub_width, centroids = book_ref.shape
    each = subs // pieces
    low = lax.broadcasted_iota(jnp.int32, (sub_width, centroids), 0) < sub_width // 2

    def write(first_ref, second_ref):
        for j in range(pieces):
            first = first_ref[j].astype(F32)
            second = second_ref[j].astype(F32)
            self_ref[j * half : (j + 1) * half, :] = first[0:half]
            neigh_ref[j * half : (j + 1) * half, :] = second[0:half]
            for e in range(each):
                at = slice(half + e * sub_width, half + (e + 1) * sub_width)
                book_ref[j * each + e] = jnp.where(low, first[at], second[at])
        row = half + sub_width // 2
        bias_ref[...] = first_ref[0].astype(F32)[row : row + 1]

    @pl.when(core == 0)
    def _():
        write(mine_ref, other_ref)

    @pl.when(core == 1)
    def _():
        write(other_ref, mine_ref)


def exchange(x, axes, groups=None):
    return lax.all_to_all(x, axes, split_axis=0, concat_axis=0, tiled=True, axis_index_groups=groups)


def body(quantizer_codes, codebook, adj_tiles, tile_list, tile_count, w_self, w_neigh, out_bias, cotangent):
    doms = lax.axis_size("dom")
    plane = lax.axis_size("tile") * lax.axis_size("rep")
    subs, centroids, sub_width = codebook.shape
    slots, side = adj_tiles.shape[1:3]
    width = subs * sub_width
    rows = side // doms
    per = slots * rows
    codes = quantizer_codes.T
    book = codebook.transpose(0, 2, 1)
    adj = adj_tiles[0]
    slot_ids = tile_list[0].T
    bias = out_bias.reshape(1, width)
    swap = [(i, i ^ 1) for i in range(doms)]
    cores = [list(range(c, doms, 2)) for c in range(2)]

    spread = jnp.broadcast_to(codes.astype(BF16)[None], (plane, subs, side))
    all_codes = exchange(spread, PLANE)
    side_rows = call(
        functools.partial(side_kernel, plane), "side", struct((doms, 2 * rows, width), BF16),
        (slot_ids, tile_count), (codes, cotangent),
    )
    parts = call(
        forward_kernel, "forward", struct((doms, per + 2 * rows, width), BF16),
        (slot_ids,), (adj, all_codes, book, side_rows), (VM((width, side), F32),),
    )
    parts = exchange(parts, DOM)
    need, dpre, agg, feats, own_codes = call(
        node_kernel, "node",
        (struct((doms, per + rows, width), BF16), struct((side, width), BF16),
         struct((side, width), BF16), struct((width, side), BF16), struct((subs, side), F32)),
        (), (parts, book, w_self, w_neigh, bias), (VM((width, side), F32),),
    )
    need = exchange(need, DOM)
    grad_self, grad_neigh, grad_bias, own_book = call(
        weights_kernel, "weights",
        (struct((width, width), F32), struct((width, width), F32), struct((sub_width, width), F32),
         struct((subs, sub_width, centroids), F32)),
        (), (feats, agg, dpre, w_self, own_codes),
    )
    piece = (width + subs * sub_width) // plane
    keep, give, node_out = call(
        backward_kernel, "backward",
        (struct((plane, piece, width), F32), struct((plane, piece, width), F32), struct((side, width), BF16)),
        (slot_ids,), (need, adj, all_codes, own_book, grad_self, grad_neigh, grad_bias),
        (VM((width, side), F32), VM((subs, sub_width, centroids), F32)),
    )
    got = lax.ppermute(give, "dom", swap)
    half = call(pair_kernel, "pair", struct((plane, piece, width), BF16), (), (keep, got))
    half = exchange(half, PLANE)
    half = call(sum_spread_kernel, "sum_plane", struct((doms // 2, piece, width), F32), (), (half,))
    half = exchange(half, "dom", cores)
    half = call(sum_spread_kernel, "sum_dom", struct((plane, piece, width), BF16), (), (half,))
    mine = exchange(half, PLANE)
    other = lax.ppermute(mine, "dom", swap)
    grad_self, grad_neigh, grad_bias, grad_book = call(
        finish_kernel, "finish",
        (struct((width, width), F32), struct((width, width), F32), struct((1, width), F32),
         struct((subs, sub_width, centroids), F32)),
        (), (mine, other),
    )
    return (node_out, grad_self, grad_neigh, grad_bias.reshape(width), grad_book.transpose(0, 2, 1))


def solution(mesh):
    every = ("dom", "tile", "rep")
    in_specs = (
        P(every, None), P(), P(every, None, None, None), P(every, None, None), P(every),
        P(), P(), P(), P(every, None),
    )
    out_specs = (P(every, None), P(), P(), P(), P())
    return jax.shard_map(body, mesh=mesh, in_specs=in_specs, out_specs=out_specs, check_vma=False)
```

time: 241 us -> 170 us (0.71)
  waiting for transfers between devices: 91.8 us -> 32.1 us
  starting transfers between devices: 44.3 us -> 21.8 us
  blocking collectives: 64.6 us -> 78.7 us
    all_to_all x8 -> x2, waiting for transfers between devices: 91.8 us -> 28.9 us  [exchange(): lax.all_to_all(x, axes, split_axis=0, concat_axis=0, tiled=True, axis_ind...]
    all_to_all x8 -> x2, starting transfers between devices: 44.3 us -> 14 us  [exchange(): lax.all_to_all(x, axes, split_axis=0, concat_axis=0, tiled=True, axis_ind...]
    all_to_all x3 -> x4, blocking collectives: 64.6 us -> 78.7 us  [exchange(): lax.all_to_all(x, axes, split_axis=0, concat_axis=0, tiled=True, axis_ind...]
    ppermute x0 -> x2, starting transfers between devices: none -> 7.81 us  [the longest x1 5.9 us: body(): other = lax.ppermute(mine, 'dom', swap)]
    ppermute x0 -> x2, waiting for transfers between devices: none -> 3.23 us  [the longest x1 2.09 us: body(): got = lax.ppermute(give, 'dom', swap)]
    pallas_call x10 -> x9, Pallas kernels: 31.4 us -> 30.2 us  [call(): pl.pallas_call(kernel, name=name, out_shape=out_shape, in_specs=[pl.Block...]
  transfers between devices with their start and end apart: 8 -> 4, of which waited for: 7 -> 4; matrix products, arithmetic and copies ran while one was open for 0% -> 0% of each run, Pallas kernels for 11% -> 4%
where the time goes in v2:
time: 170 us; the launch traced here: 169 us
  blocking collectives  78.7 us (46%)
  waiting for transfers between devices  32.1 us (19%)
  Pallas kernels  30.2 us (18%)
  starting transfers between devices  21.8 us (13%)
  local copies, waits for them, and re-layouts  4.01 us (2%)
    all_to_all x4, blocking collectives, exchange(): lax.all_to_all(x, axes, split_axis=0, concat_axis=0, tiled=True, axis_ind...  78.7 us
    pallas_call x9, Pallas kernels, call(): pl.pallas_call(kernel, name=name, out_shape=out_shape, in_specs=[pl.Block...  30.2 us
    all_to_all x2, waiting for transfers between devices, exchange(): lax.all_to_all(x, axes, split_axis=0, concat_axis=0, tiled=True, axis_ind...  28.9 us
    all_to_all x2, starting transfers between devices, exchange(): lax.all_to_all(x, axes, split_axis=0, concat_axis=0, tiled=True, axis_ind...  14 us
    ppermute x1, starting transfers between devices, body(): other = lax.ppermute(mine, 'dom', swap)  5.9 us
  transfers between devices with their start and end apart: 4, of which 4 were waited for; matrix products, arithmetic and copies ran while one was open for 0% of the time, Pallas kernels for 4%

profile of v2, /device:TPU:1, one launch (start us, length us, event | category | flops | bytes accessed | tf_op | source)
XLA Modules:
  0.0 169.0 jit_solution(1670262811078075889)
XLA Ops:
  1.4 0.9 broadcast_in_dim.2
  2.2 10.5 %all-to-all-start = ((bf16[32,32,256]{2,1,0:T(8,128)(2,1)}), bf16[32,32,256]{2,1,0:T(8,128)(2,1)S(1)}, u32[]{:S(2)}, u32[]{:S(2)}) async-start(bf16[32,32,256]{2,1,0:T(8,128)(2,1)} %broadcast_in_dim.2), calls=%async_computation | async-start | bytes 1048576 | tf_op jit(solution)/shard_map/all_to_all | solution.py:256
  13.4 1.8 %side.1.side_ref = bf16[16,32,256]{2,1,0:T(8,128)(2,1)} custom-call(s32[2,4]{1,0:T(2,128)} %bitcast.15, s32[1]{0:T(128)S(6)} %copy.14.tc_ref, s32[32,256]{1,0:T(8,128)} %bitcast.14, bf16[256,256]{1,0:T(8,128)(2,1)} %cot_ref.1), custom_call_target="tpu_custom_call" | custom-call | tf_op jit(solution)/shard_map/side/pallas_call | solution.py:23
  15.2 13.8 %all-to-all-done.codes_ref = bf16[32,32,256]{2,1,0:T(8,128)(2,1)S(1)} async-done(((bf16[32,32,256]{2,1,0:T(8,128)(2,1)}), bf16[32,32,256]{2,1,0:T(8,128)(2,1)S(1)}, u32[]{:S(2)}, u32[]{:S(2)}) %all-to-all-start) | async-done | bytes 524320 | tf_op jit(solution)/shard_map/all_to_all | solution.py:256
  29.0 0.8 copy-done
  29.8 5.1 %forward.1 = bf16[16,96,256]{2,1,0:T(8,128)(2,1)} custom-call(s32[2,4]{1,0:T(2,128)} %bitcast.16, bf16[4,256,256]{2,1,0:T(8,128)(2,1)} %bitcast.10, bf16[32,32,256]{2,1,0:T(8,128)(2,1)} %copy-done, bf16[32,8,256]{2,1,0:T(8,128)(2,1)} %bitcast.12, bf16[16,32,256]{2,1,0:T(8,128)(2,1)} %side.1.side_ref), custom_call_target="tpu_custom_call" | custom-call | tf_op jit(solution)/shard_map/forward/pallas_call | solution.py:23
  34.9 35.7 %all_to_all.30.got_ref = bf16[16,96,256]{2,1,0:T(8,128)(2,1)} all-to-all(bf16[16,96,256]{2,1,0:T(8,128)(2,1)} %forward.1), channel_id=1, replica_groups=mesh['dom'=16,'tile'=8,'rep'=4] {'dom'}, dimensions={0} | all-to-all | bytes 1572864 | tf_op jit(solution)/shard_map/all_to_all | solution.py:256
  70.6 4.4 %node.1 = (bf16[16,80,256]{2,1,0:T(8,128)(2,1)}, bf16[256,256]{1,0:T(8,128)(2,1)}, bf16[256,256]{1,0:T(8,128)(2,1)}, bf16[256,256]{1,0:T(8,128)(2,1)}, f32[32,256]{1,0:T(8,128)}) custom-call(bf16[16,96,256]{2,1,0:T(8,128)(2,1)} %all_to_all.30.got_ref, bf16[32,8,256]{2,1,0:T(8,128)(2,1)} %bitcast.13, bf16[256,256]{1,0:T(8,128)(2,1)} %w_ref.1, ...), custom_call_target="tpu_custom_call" | custom-call | tf_op jit(solution)/shard_map/node/pallas_call | solution.py:23
  75.0 3.5 %all-to-all-start.2 = ((bf16[16,80,256]{2,1,0:T(8,128)(2,1)}), bf16[16,80,256]{2,1,0:T(8,128)(2,1)S(1)}, u32[]{:S(2)}, u32[]{:S(2)}) async-start(bf16[16,80,256]{2,1,0:T(8,128)(2,1)} %get-tuple-element.21), calls=%async_computation.2 | async-start | bytes 1310720 | tf_op jit(solution)/shard_map/all_to_all | solution.py:256
  78.5 4.3 %weights.1 = (f32[256,256]{1,0:T(8,128)}, f32[256,256]{1,0:T(8,128)}, f32[8,256]{1,0:T(8,128)}, f32[32,8,256]{2,1,0:T(8,128)}) custom-call(bf16[256,256]{1,0:T(8,128)(2,1)} %get-tuple-element.22.feats_ref, bf16[256,256]{1,0:T(8,128)(2,1)} %get-tuple-element.23.agg_ref, bf16[256,256]{1,0:T(8,128)(2,1)} %get-tuple-element.24.dpre_ref, bf16[256,256]{1,0:T(8,128)(2,1)} %w_ref.1, ...), custom_call_target="tpu_custom_call" | custom-call | tf_op jit(solution)/shard_map/weights/pallas_call | solution.py:23
  82.7 15.1 %all-to-all-done.2.got_ref = bf16[16,80,256]{2,1,0:T(8,128)(2,1)S(1)} async-done(((bf16[16,80,256]{2,1,0:T(8,128)(2,1)}), bf16[16,80,256]{2,1,0:T(8,128)(2,1)S(1)}, u32[]{:S(2)}, u32[]{:S(2)}) %all-to-all-start.2) | async-done | bytes 655392 | tf_op jit(solution)/shard_map/all_to_all | solution.py:256
  97.8 0.9 copy-done.1
  98.7 7.5 %backward.1 = (f32[32,16,256]{2,1,0:T(8,128)}, f32[32,16,256]{2,1,0:T(8,128)}, bf16[256,256]{1,0:T(8,128)(2,1)}) custom-call(s32[2,4]{1,0:T(2,128)} %bitcast.17, bf16[16,80,256]{2,1,0:T(8,128)(2,1)} %copy-done.1, bf16[4,256,256]{2,1,0:T(8,128)(2,1)} %bitcast.11, bf16[32,32,256]{2,1,0:T(8,128)(2,1)} %copy-done, f32[32,8,256]{2,1,0:T(8,128)} %get-tuple-element.26.own_ref, ...), custom_call_target="tpu_custom_call" | custom-call | tf_op jit(solution)/shard_map/backward/pallas_call | solution.py:23
  106.2 1.9 %collective-permute-start = (f32[32,16,256]{2,1,0:T(8,128)}, f32[32,16,256]{2,1,0:T(8,128)S(1)}, u32[]{:S(2)}, u32[]{:S(2)}) collective-permute-start(f32[32,16,256]{2,1,0:T(8,128)} %get-tuple-element.32), channel_id=1, source_target_pairs={{0,32},{32,0},{64,96},{96,64},{128,160},{160,128},{192,224},{224,1... | collective-permute-start | bytes 1572872 | tf_op jit(solution)/shard_map/ppermute | solution.py:306
  108.1 2.1 %collective-permute-done.got_ref = f32[32,16,256]{2,1,0:T(8,128)S(1)} collective-permute-done((f32[32,16,256]{2,1,0:T(8,128)}, f32[32,16,256]{2,1,0:T(8,128)S(1)}, u32[]{:S(2)}, u32[]{:S(2)}) %collective-permute-start) | collective-permute-done | bytes 524320 | tf_op jit(solution)/shard_map/ppermute | solution.py:306
  111.0 1.9 %pair.1 = bf16[32,16,256]{2,1,0:T(8,128)(2,1)} custom-call(f32[32,16,256]{2,1,0:T(8,128)} %get-tuple-element.31.keep_ref, f32[32,16,256]{2,1,0:T(8,128)} %copy-done.3), custom_call_target="tpu_custom_call" | custom-call | tf_op jit(solution)/shard_map/pair/pallas_call | solution.py:23
  112.9 16.4 %all_to_all.31.in_ref = bf16[32,16,256]{2,1,0:T(8,128)(2,1)} all-to-all(bf16[32,16,256]{2,1,0:T(8,128)(2,1)} %pair.1), channel_id=1, replica_groups=mesh['dom'=16,'tile'=8,'rep'=4] {'tile','rep'}, dimensions={0} | all-to-all | bytes 524288 | tf_op jit(solution)/shard_map/all_to_all | solution.py:256
  129.3 1.7 sum_plane.1
  131.0 12.0 %all_to_all.32.in_ref = f32[8,16,256]{2,1,0:T(8,128)} all-to-all(f32[8,16,256]{2,1,0:T(8,128)} %sum_plane.1), channel_id=1, replica_groups={{0,64,128,192,256,320,384,448},{32,96,160,224,288,352,416,480},{1,65,12..., dimensions={0} | all-to-all | bytes 262144 | tf_op jit(solution)/shard_map/all_to_all | solution.py:256
  143.0 1.6 sum_dom.1
  144.6 14.6 %all_to_all.33.mine_ref = bf16[32,16,256]{2,1,0:T(8,128)(2,1)S(1)} all-to-all(bf16[32,16,256]{2,1,0:T(8,128)(2,1)} %sum_dom.1), channel_id=1, replica_groups=mesh['dom'=16,'tile'=8,'rep'=4] {'tile','rep'}, dimensions={0} | all-to-all | bytes 524288 | tf_op jit(solution)/shard_map/all_to_all | solution.py:256
  159.3 5.9 %collective-permute-start.1 = (bf16[32,16,256]{2,1,0:T(8,128)(2,1)S(1)}, bf16[32,16,256]{2,1,0:T(8,128)(2,1)S(1)}, u32[]{:S(2)}, u32[]{:S(2)}) collective-permute-start(bf16[32,16,256]{2,1,0:T(8,128)(2,1)S(1)} %all_to_all.33.mine_ref), channel_id=1, source_target_pairs={{0,32},{32,0},{64,96},{96,64},{128,160},{160,128},{192,224},{224,1... | collective-permute-start | bytes 786440 | tf_op jit(solution)/shard_map/ppermute | solution.py:313
  165.2 1.1 collective-permute-done.1.other_ref
  167.0 2.0 %finish.1 = (f32[256,256]{1,0:T(8,128)}, f32[256,256]{1,0:T(8,128)}, f32[1,256]{1,0:T(1,128)}, f32[32,8,256]{2,1,0:T(8,128)}) custom-call(bf16[32,16,256]{2,1,0:T(8,128)(2,1)} %copy-done.2, bf16[32,16,256]{2,1,0:T(8,128)(2,1)} %copy-done.4), custom_call_target="tpu_custom_call" | custom-call | tf_op jit(solution)/shard_map/finish/pallas_call | solution.py:23
  (9 shorter events, 2.3 us)
Async XLA Ops:
  2.2 26.8 %all-to-all-start = ((bf16[32,32,256]{2,1,0:T(8,128)(2,1)}), bf16[32,32,256]{2,1,0:T(8,128)(2,1)S(1)}, u32[]{:S(2)}, u32[]{:S(2)}) async-start(bf16[32,32,256]{2,1,0:T(8,128)(2,1)} %broadcast_in_dim.2), calls=%async_computation | async-start | bytes 1048576 | tf_op jit(solution)/shard_map/all_to_all | solution.py:256
  29.0 0.8 copy-start
  75.0 22.9 %all-to-all-start.2 = ((bf16[16,80,256]{2,1,0:T(8,128)(2,1)}), bf16[16,80,256]{2,1,0:T(8,128)(2,1)S(1)}, u32[]{:S(2)}, u32[]{:S(2)}) async-start(bf16[16,80,256]{2,1,0:T(8,128)(2,1)} %get-tuple-element.21), calls=%async_computation.2 | async-start | bytes 1310720 | tf_op jit(solution)/shard_map/all_to_all | solution.py:256
  97.8 0.9 copy-start.1
  106.2 4.0 %collective-permute-start = (f32[32,16,256]{2,1,0:T(8,128)}, f32[32,16,256]{2,1,0:T(8,128)S(1)}, u32[]{:S(2)}, u32[]{:S(2)}) collective-permute-start(f32[32,16,256]{2,1,0:T(8,128)} %get-tuple-element.32), channel_id=1, source_target_pairs={{0,32},{32,0},{64,96},{96,64},{128,160},{160,128},{192,224},{224,1... | collective-permute-start | bytes 1572872 | tf_op jit(solution)/shard_map/ppermute | solution.py:306
  110.2 0.8 copy-start.3
  159.3 7.1 %copy-start.2 = (bf16[32,16,256]{2,1,0:T(8,128)(2,1)}, bf16[32,16,256]{2,1,0:T(8,128)(2,1)S(1)}, u32[]{:S(2)}) copy-start(bf16[32,16,256]{2,1,0:T(8,128)(2,1)S(1)} %all_to_all.33.mine_ref) | copy-start | bytes 786436
  159.3 7.0 %collective-permute-start.1 = (bf16[32,16,256]{2,1,0:T(8,128)(2,1)S(1)}, bf16[32,16,256]{2,1,0:T(8,128)(2,1)S(1)}, u32[]{:S(2)}, u32[]{:S(2)}) collective-permute-start(bf16[32,16,256]{2,1,0:T(8,128)(2,1)S(1)} %all_to_all.33.mine_ref), channel_id=1, source_target_pairs={{0,32},{32,0},{64,96},{96,64},{128,160},{160,128},{192,224},{224,1... | collective-permute-start | bytes 786440 | tf_op jit(solution)/shard_map/ppermute | solution.py:313
  166.3 0.7 copy-start.4

commit v3 on v2

--- a/solution.py
+++ b/solution.py
@@ -11,6 +11,7 @@
 F32 = jnp.float32
 BF16 = jnp.bfloat16
 VM = pltpu.VMEM
+VMEM_LIMIT = 16 << 20
 DOM = ("dom",)
 PLANE = ("tile", "rep")
 
@@ -19,7 +20,13 @@
     return lax.dot_general(a, b, (((da,), (db,)), ((), ())), preferred_element_type=F32)
 
 
-def call(kernel, name, out_shape, scalars, arrays, scratch=()):
+def call(kernel, name, out_shape, scalars, arrays, scratch=(), final=0):
+    if not INTERPRET:
+        arrays = [pltpu.with_memory_space_constraint(a, VM) for a in arrays]
+        shapes = out_shape if isinstance(out_shape, tuple) else (out_shape,)
+        kept = len(shapes) - final
+        shapes = tuple(VM(o.shape, o.dtype) if i < kept else o for i, o in enumerate(shapes))
+        out_shape = shapes if isinstance(out_shape, tuple) else shapes[0]
     return pl.pallas_call(
         kernel,
         name=name,
@@ -28,6 +35,7 @@
         + [pl.BlockSpec(memory_space=VM)] * len(arrays),
         out_specs=jax.tree.map(lambda _: pl.BlockSpec(memory_space=VM), out_shape),
         scratch_shapes=list(scratch),
+        compiler_params=pltpu.CompilerParams(vmem_limit_bytes=VMEM_LIMIT),
         interpret=INTERPRET,
     )(*scalars, *arrays)
 
@@ -37,7 +45,7 @@
 
 
 def onehot(row, centroid_ids):
-    return jnp.where(centroid_ids == row, 1.0, 0.0).astype(BF16)
+    return jnp.where(centroid_ids.astype(BF16) == row.astype(BF16), jnp.ones((), BF16), jnp.zeros((), BF16))
 
 
 def centroid_iota(centroids, nodes):
@@ -301,7 +309,7 @@
         backward_kernel, "backward",
         (struct((plane, piece, width), F32), struct((plane, piece, width), F32), struct((side, width), BF16)),
         (slot_ids,), (need, adj, all_codes, own_book, grad_self, grad_neigh, grad_bias),
-        (VM((width, side), F32), VM((subs, sub_width, centroids), F32)),
+        (VM((width, side), F32), VM((subs, sub_width, centroids), F32)), 1,
     )
     got = lax.ppermute(give, "dom", swap)
     half = call(pair_kernel, "pair", struct((plane, piece, width), BF16), (), (keep, got))
@@ -315,7 +323,7 @@
         finish_kernel, "finish",
         (struct((width, width), F32), struct((width, width), F32), struct((1, width), F32),
          struct((subs, sub_width, centroids), F32)),
-        (), (mine, other),
+        (), (mine, other), (), 4,
     )
     return (node_out, grad_self, grad_neigh, grad_bias.reshape(width), grad_book.transpose(0, 2, 1))
 

time: 170 us -> 154 us (0.906)
  Pallas kernels: 30.2 us -> 16.9 us
  blocking collectives: 78.7 us -> 76.2 us
  waiting for transfers between devices: 32.1 us -> 34.1 us
  local copies, waits for them, and re-layouts: 4.01 us -> 2.21 us
    pallas_call x9, Pallas kernels: 30.2 us -> 16.9 us  [call(): pl.pallas_call(kernel, name=name, out_shape=out_shape, in_specs=[pl.Block...]
    all_to_all x4, blocking collectives: 78.7 us -> 76.2 us  [exchange(): lax.all_to_all(x, axes, split_axis=0, concat_axis=0, tiled=True, axis_ind...]
    all_to_all x2, waiting for transfers between devices: 28.9 us -> 31.1 us  [exchange(): lax.all_to_all(x, axes, split_axis=0, concat_axis=0, tiled=True, axis_ind...]
    unnamed x10 -> x16, local copies, waits for them, and re-layouts: 3.16 us -> 1.36 us
  transfers between devices with their start and end apart: 4 -> 4, of which waited for: 4 -> 4; matrix products, arithmetic and copies ran while one was open for 0% -> 0% of each run, Pallas kernels for 4% -> 2%
where the time goes in v3:
time: 154 us
  blocking collectives  76.2 us (49%)
  waiting for transfers between devices  34.1 us (22%)
  starting transfers between devices  22.1 us (14%)
  Pallas kernels  16.9 us (11%)
  local copies, waits for them, and re-layouts  2.21 us (1%)
    all_to_all x4, blocking collectives, exchange(): lax.all_to_all(x, axes, split_axis=0, concat_axis=0, tiled=True, axis_ind...  76.2 us
    all_to_all x2, waiting for transfers between devices, exchange(): lax.all_to_all(x, axes, split_axis=0, concat_axis=0, tiled=True, axis_ind...  31.1 us
    pallas_call x9, Pallas kernels, call(): pl.pallas_call(kernel, name=name, out_shape=out_shape, in_specs=[pl.Block...  16.9 us
    all_to_all x2, starting transfers between devices, exchange(): lax.all_to_all(x, axes, split_axis=0, concat_axis=0, tiled=True, axis_ind...  14.1 us
    ppermute x1, starting transfers between devices, body(): other = lax.ppermute(mine, 'dom', swap)  6.11 us
  transfers between devices with their start and end apart: 4, of which 4 were waited for; matrix products, arithmetic and copies ran while one was open for 0% of the time, Pallas kernels for 2%

profile of v3, /device:TPU:1, one launch (start us, length us, event | category | flops | bytes accessed | tf_op | source)
XLA Modules:
  0.0 153.7 jit_solution(10925648379341500599)
XLA Ops:
  0.6 0.8 bitcast_convert_fusion
  1.4 0.9 broadcast_in_dim.2
  2.3 10.6 %all-to-all-start = ((bf16[32,32,256]{2,1,0:T(8,128)(2,1)}), bf16[32,32,256]{2,1,0:T(8,128)(2,1)S(1)}, u32[]{:S(2)}, u32[]{:S(2)}) async-start(bf16[32,32,256]{2,1,0:T(8,128)(2,1)} %broadcast_in_dim.2), calls=%async_computation | async-start | bytes 1048576 | tf_op jit(solution)/shard_map/all_to_all | solution.py:264
  13.6 0.7 copy-done.6
  14.2 0.7 side.1.side_ref
  15.0 14.2 %all-to-all-done.codes_ref = bf16[32,32,256]{2,1,0:T(8,128)(2,1)S(1)} async-done(((bf16[32,32,256]{2,1,0:T(8,128)(2,1)}), bf16[32,32,256]{2,1,0:T(8,128)(2,1)S(1)}, u32[]{:S(2)}, u32[]{:S(2)}) %all-to-all-start) | async-done | bytes 524320 | tf_op jit(solution)/shard_map/all_to_all | solution.py:264
  29.2 3.4 %forward.1 = bf16[16,96,256]{2,1,0:T(8,128)(2,1)S(1)} custom-call(s32[2,4]{1,0:T(2,128)S(1)} %bitcast.16, bf16[4,256,256]{2,1,0:T(8,128)(2,1)S(1)} %bitcast.10, bf16[32,32,256]{2,1,0:T(8,128)(2,1)S(1)} %all-to-all-done.codes_ref, bf16[32,8,256]{2,1,0:T(8,128)(2,1)S(1)} %bitcast.12, bf16[16,32,256]{2,1,0:T(8,128)(2,1)S(1)} %side.1.side_ref), custom_call_target="tpu_custom_call" | custom-call | tf_op jit(solution)/shard_map/forward/pallas_call | solution.py:30
  32.6 35.5 %all_to_all.30.got_ref = bf16[16,96,256]{2,1,0:T(8,128)(2,1)S(1)} all-to-all(bf16[16,96,256]{2,1,0:T(8,128)(2,1)S(1)} %forward.1), channel_id=1, replica_groups=mesh['dom'=16,'tile'=8,'rep'=4] {'dom'}, dimensions={0} | all-to-all | bytes 1572864 | tf_op jit(solution)/shard_map/all_to_all | solution.py:264
  68.1 0.7 copy-done.7
  68.8 3.1 %node.1 = (bf16[16,80,256]{2,1,0:T(8,128)(2,1)}, bf16[256,256]{1,0:T(8,128)(2,1)S(1)}, bf16[256,256]{1,0:T(8,128)(2,1)S(1)}, bf16[256,256]{1,0:T(8,128)(2,1)S(1)}, f32[32,256]{1,0:T(8,128)S(1)}) custom-call(bf16[16,96,256]{2,1,0:T(8,128)(2,1)S(1)} %all_to_all.30.got_ref, bf16[32,8,256]{2,1,0:T(8,128)(2,1)S(1)} %bitcast.13, bf16[256,256]{1,0:T(8,128)(2,1)S(1)} %copy-done.2, ...), custom_call_target="tpu_custom_call" | custom-call | tf_op jit(solution)/shard_map/node/pallas_call | solution.py:30
  71.9 3.5 %all-to-all-start.2 = ((bf16[16,80,256]{2,1,0:T(8,128)(2,1)}), bf16[16,80,256]{2,1,0:T(8,128)(2,1)S(1)}, u32[]{:S(2)}, u32[]{:S(2)}) async-start(bf16[16,80,256]{2,1,0:T(8,128)(2,1)} %get-tuple-element.21), calls=%async_computation.2 | async-start | bytes 1310720 | tf_op jit(solution)/shard_map/all_to_all | solution.py:264
  75.4 2.4 %weights.1 = (f32[256,256]{1,0:T(8,128)S(1)}, f32[256,256]{1,0:T(8,128)S(1)}, f32[8,256]{1,0:T(8,128)S(1)}, f32[32,8,256]{2,1,0:T(8,128)S(1)}) custom-call(bf16[256,256]{1,0:T(8,128)(2,1)S(1)} %get-tuple-element.22.feats_ref, bf16[256,256]{1,0:T(8,128)(2,1)S(1)} %get-tuple-element.23.agg_ref, bf16[256,256]{1,0:T(8,128)(2,1)S(1)} %get-tuple-element.24.dpre_ref, ...), custom_call_target="tpu_custom_call" | custom-call | tf_op jit(solution)/shard_map/weights/pallas_call | solution.py:30
  77.8 16.9 %all-to-all-done.2.got_ref = bf16[16,80,256]{2,1,0:T(8,128)(2,1)S(1)} async-done(((bf16[16,80,256]{2,1,0:T(8,128)(2,1)}), bf16[16,80,256]{2,1,0:T(8,128)(2,1)S(1)}, u32[]{:S(2)}, u32[]{:S(2)}) %all-to-all-start.2) | async-done | bytes 655392 | tf_op jit(solution)/shard_map/all_to_all | solution.py:264
  94.8 6.1 %backward.1 = (f32[32,16,256]{2,1,0:T(8,128)S(1)}, f32[32,16,256]{2,1,0:T(8,128)S(1)}, bf16[256,256]{1,0:T(8,128)(2,1)}) custom-call(s32[2,4]{1,0:T(2,128)S(1)} %bitcast.17, bf16[16,80,256]{2,1,0:T(8,128)(2,1)S(1)} %all-to-all-done.2.got_ref, bf16[4,256,256]{2,1,0:T(8,128)(2,1)S(1)} %bitcast.11, bf16[32,32,256]{2,1,0:T(8,128)(2,1)S(1)} %all-to-all-done.codes_ref, ...), custom_call_target="tpu_custom_call" | custom-call | tf_op jit(solution)/shard_map/backward/pallas_call | solution.py:30
  100.8 1.9 %collective-permute-start = (f32[32,16,256]{2,1,0:T(8,128)S(1)}, f32[32,16,256]{2,1,0:T(8,128)S(1)}, u32[]{:S(2)}, u32[]{:S(2)}) collective-permute-start(f32[32,16,256]{2,1,0:T(8,128)S(1)} %get-tuple-element.32), channel_id=1, source_target_pairs={{0,32},{32,0},{64,96},{96,64},{128,160},{160,128},{192,224},{224,1... | collective-permute-start | bytes 1572872 | tf_op jit(solution)/shard_map/ppermute | solution.py:314
  102.7 1.9 %collective-permute-done.got_ref = f32[32,16,256]{2,1,0:T(8,128)S(1)} collective-permute-done((f32[32,16,256]{2,1,0:T(8,128)S(1)}, f32[32,16,256]{2,1,0:T(8,128)S(1)}, u32[]{:S(2)}, u32[]{:S(2)}) %collective-permute-start) | collective-permute-done | bytes 524320 | tf_op jit(solution)/shard_map/ppermute | solution.py:314
  104.6 0.1 pair.1
  104.7 15.8 %all_to_all.31.in_ref = bf16[32,16,256]{2,1,0:T(8,128)(2,1)S(1)} all-to-all(bf16[32,16,256]{2,1,0:T(8,128)(2,1)S(1)} %pair.1), channel_id=1, replica_groups=mesh['dom'=16,'tile'=8,'rep'=4] {'tile','rep'}, dimensions={0} | all-to-all | bytes 524288 | tf_op jit(solution)/shard_map/all_to_all | solution.py:264
  120.5 0.1 sum_plane.1
  120.6 10.4 %all_to_all.32.in_ref = f32[8,16,256]{2,1,0:T(8,128)S(1)} all-to-all(f32[8,16,256]{2,1,0:T(8,128)S(1)} %sum_plane.1), channel_id=1, replica_groups={{0,64,128,192,256,320,384,448},{32,96,160,224,288,352,416,480},{1,65,12..., dimensions={0} | all-to-all | bytes 262144 | tf_op jit(solution)/shard_map/all_to_all | solution.py:264
  131.0 14.5 %all_to_all.33.mine_ref = bf16[32,16,256]{2,1,0:T(8,128)(2,1)S(1)} all-to-all(bf16[32,16,256]{2,1,0:T(8,128)(2,1)S(1)} %sum_dom.1), channel_id=1, replica_groups=mesh['dom'=16,'tile'=8,'rep'=4] {'tile','rep'}, dimensions={0} | all-to-all | bytes 524288 | tf_op jit(solution)/shard_map/all_to_all | solution.py:264
  145.5 6.1 %collective-permute-start.1 = (bf16[32,16,256]{2,1,0:T(8,128)(2,1)S(1)}, bf16[32,16,256]{2,1,0:T(8,128)(2,1)S(1)}, u32[]{:S(2)}, u32[]{:S(2)}) collective-permute-start(bf16[32,16,256]{2,1,0:T(8,128)(2,1)S(1)} %all_to_all.33.mine_ref), channel_id=1, source_target_pairs={{0,32},{32,0},{64,96},{96,64},{128,160},{160,128},{192,224},{224,1... | collective-permute-start | bytes 786440 | tf_op jit(solution)/shard_map/ppermute | solution.py:321
  151.6 1.1 collective-permute-done.1.other_ref
  152.7 0.9 finish.1
  (15 shorter events, 0.1 us)
Async XLA Ops:
  2.2 11.3 %copy-start.3 = (bf16[256,256]{1,0:T(8,128)(2,1)S(1)}, bf16[256,256]{1,0:T(8,128)(2,1)}, u32[]{:S(2)}) copy-start(bf16[256,256]{1,0:T(8,128)(2,1)} %cot_ref.1) | copy-start | bytes 393220
  2.2 11.3 %copy-start.4 = (s32[256,32]{0,1:T(8,128)S(1)}, s32[256,32]{0,1:T(8,128)}, u32[]{:S(2)}) copy-start(s32[256,32]{0,1:T(8,128)} %param.9) | copy-start | bytes 98308
  2.3 26.9 %copy-start = (bf16[1,4,256,256]{3,2,1,0:T(8,128)(2,1)S(1)}, bf16[1,4,256,256]{3,2,1,0:T(8,128)(2,1)}, u32[]{:S(2)}) copy-start(bf16[1,4,256,256]{3,2,1,0:T(8,128)(2,1)} %param.11) | copy-start | bytes 1572868
  2.3 26.9 %all-to-all-start = ((bf16[32,32,256]{2,1,0:T(8,128)(2,1)}), bf16[32,32,256]{2,1,0:T(8,128)(2,1)S(1)}, u32[]{:S(2)}, u32[]{:S(2)}) async-start(bf16[32,32,256]{2,1,0:T(8,128)(2,1)} %broadcast_in_dim.2), calls=%async_computation | async-start | bytes 1048576 | tf_op jit(solution)/shard_map/all_to_all | solution.py:264
  13.5 0.7 copy-start.6
  14.2 15.0 %copy-start.1 = (bf16[32,256,8]{1,2,0:T(8,128)(2,1)S(1)}, bf16[32,256,8]{1,2,0:T(8,128)(2,1)}, u32[]{:S(2)}) copy-start(bf16[32,256,8]{1,2,0:T(8,128)(2,1)} %param.10) | copy-start | bytes 393220
  32.6 35.5 %copy-start.2 = (bf16[256,256]{1,0:T(8,128)(2,1)S(1)}, bf16[256,256]{1,0:T(8,128)(2,1)}, u32[]{:S(2)}) copy-start(bf16[256,256]{1,0:T(8,128)(2,1)} %w_ref.1) | copy-start | bytes 393220
  32.6 35.5 %copy-start.5 = (bf16[256,256]{1,0:T(8,128)(2,1)S(1)}, bf16[256,256]{1,0:T(8,128)(2,1)}, u32[]{:S(2)}) copy-start(bf16[256,256]{1,0:T(8,128)(2,1)} %wneigh_ref.1) | copy-start | bytes 393220
  68.1 0.7 copy-start.7
  71.9 22.9 %all-to-all-start.2 = ((bf16[16,80,256]{2,1,0:T(8,128)(2,1)}), bf16[16,80,256]{2,1,0:T(8,128)(2,1)S(1)}, u32[]{:S(2)}, u32[]{:S(2)}) async-start(bf16[16,80,256]{2,1,0:T(8,128)(2,1)} %get-tuple-element.21), calls=%async_computation.2 | async-start | bytes 1310720 | tf_op jit(solution)/shard_map/all_to_all | solution.py:264
  100.8 3.8 %collective-permute-start = (f32[32,16,256]{2,1,0:T(8,128)S(1)}, f32[32,16,256]{2,1,0:T(8,128)S(1)}, u32[]{:S(2)}, u32[]{:S(2)}) collective-permute-start(f32[32,16,256]{2,1,0:T(8,128)S(1)} %get-tuple-element.32), channel_id=1, source_target_pairs={{0,32},{32,0},{64,96},{96,64},{128,160},{160,128},{192,224},{224,1... | collective-permute-start | bytes 1572872 | tf_op jit(solution)/shard_map/ppermute | solution.py:314
  145.5 7.3 %collective-permute-start.1 = (bf16[32,16,256]{2,1,0:T(8,128)(2,1)S(1)}, bf16[32,16,256]{2,1,0:T(8,128)(2,1)S(1)}, u32[]{:S(2)}, u32[]{:S(2)}) collective-permute-start(bf16[32,16,256]{2,1,0:T(8,128)(2,1)S(1)} %all_to_all.33.mine_ref), channel_id=1, source_target_pairs={{0,32},{32,0},{64,96},{96,64},{128,160},{160,128},{192,224},{224,1... | collective-permute-start | bytes 786440 | tf_op jit(solution)/shard_map/ppermute | solution.py:321
